TPU v7x, 128 devices: a whole 4x4x4 slice. The times are simulated.
128 devices in a mesh: lang: 8 (over z, y_lo), fsdp: 16 (over y_hi, x, core).
Axes of the slice: x: 4, y: 4 (y_hi: 2, y_lo: 2; y = y_hi * 2 + y_lo), z: 4, core: 2. Of those that a mesh axis runs over, the one named last changes fastest.
Arguments:
- tokens: bfloat16 [8, 768, 8192], P('lang', 'fsdp'), may hold values from -6 to 6
- grad_out: bfloat16 [8, 768, 8192], P('lang', 'fsdp'), may hold values from -24 to 24
- doc_ids: int32 [8, 768], P('lang'), may hold values from 0 to 95, never falling along the last dimension, each value on 1 to 64 neighbouring positions
- w_gate: bfloat16 [8192, 4096], P(None, 'fsdp'), may hold values from -0.0625 to 0.0625
- w_up: bfloat16 [8192, 4096], P(None, 'fsdp'), may hold values from -0.0625 to 0.0625
- w_down: bfloat16 [4096, 8192], P('fsdp'), may hold values from -0.09375 to 0.09375
Outputs:
- grad_tokens: bfloat16 [8, 768, 8192], P('lang', 'fsdp')
- grad_gate: bfloat16 [8192, 4096], P('lang', 'fsdp')
- grad_up: bfloat16 [8192, 4096], P('lang', 'fsdp')
- grad_down: bfloat16 [4096, 8192], P('fsdp', 'lang')
Inputs may be any that keep to these rules, and one draw needn't show every extreme that they name: `doc_ids`: document numbers never fall along a group's pack.
All inputs are finite; a program needn't handle non-finite values.
Results may differ from a plain program's by a relative error of at most 0.015.
Values may be sent and summed in bfloat16 or wider, within the bound.
No kernel may reach another device: no remote copies, remote signals or barrier semaphores. Data moves between devices by JAX's collectives and lax.ppermute only.
A program may use at most 192 MiB of HBM per device.

v0:
```python
import jax
import jax.numpy as jnp
from jax import lax
from jax.sharding import PartitionSpec as P

epsilon = 1e-06


def sent_together(arrays, axis, dim, along):
    both = jnp.concatenate(arrays, axis=along)
    filled, at, gathered = (lax.all_gather(both, axis, axis=dim, tiled=True), 0, [])
    for a in arrays:
        gathered.append(lax.slice_in_dim(filled, at, at + a.shape[along], axis=along))
        at += a.shape[along]
    return tuple(gathered)


def copy_for_each(value, axis):
    length = lax.axis_size(axis)
    return lax.all_to_all(
        jnp.broadcast_to(value[None], (length, *value.shape)), axis, 0, 0, tiled=True
    )


def taken_together(value, axis):
    return copy_for_each(value, axis).sum(axis=0)


def contract_rows(left, right):
    return lax.dot_general(
        left, right, (((0,), (0,)), ((), ())), preferred_element_type=jnp.float32
    )


def contract_cols(left, right):
    return lax.dot_general(
        left, right, (((1,), (1,)), ((), ())), preferred_element_type=jnp.float32
    )


def body(tokens, grad_out, doc_ids, w_gate, w_up, w_down):
    features, upstream = sent_together((tokens, grad_out), "fsdp", 1, 0)
    features = features[0]
    upstream = upstream[0]
    segment = doc_ids[0]
    width = features.shape[1]
    counts = jnp.sum((segment[:, None] == segment[None, :]).astype(jnp.float32), axis=1)
    inverse = 1.0 / counts
    gate_pre = jnp.dot(features, w_gate, preferred_element_type=jnp.float32)
    up_pre = jnp.dot(features, w_up, preferred_element_type=jnp.float32)
    gate_sig = jax.nn.sigmoid(gate_pre)
    activated = gate_pre * gate_sig
    hidden = (activated * up_pre * inverse[:, None]).astype(jnp.bfloat16)
    hid_grad = contract_cols(upstream, w_down) * inverse[:, None]
    gate_grad = (hid_grad * up_pre * gate_sig * (1.0 + gate_pre * (1.0 - gate_sig))).astype(
        jnp.bfloat16
    )
    up_grad = (hid_grad * activated).astype(jnp.bfloat16)
    stacked = jnp.stack(
        [
            contract_rows(features, gate_grad),
            contract_rows(features, up_grad),
            contract_rows(upstream, hidden),
        ]
    )
    moment = jnp.sum(stacked * stacked, axis=(0, 1)) / (3.0 * width) + epsilon
    ratios = 1.0 / moment
    summed_ratio = taken_together(ratios, "lang")
    weighted = stacked * (ratios / summed_ratio)[None, None, :]
    pieces = lax.all_to_all(
        weighted.astype(jnp.bfloat16)[None], "lang", split_axis=2, concat_axis=0, tiled=True
    )
    shares = jnp.sum(pieces, axis=0, dtype=jnp.float32)
    grad_gate = shares[0].astype(jnp.bfloat16)
    grad_up = shares[1].astype(jnp.bfloat16)
    grad_down = shares[2].T.astype(jnp.bfloat16)
    summed = lax.psum_scatter(
        (contract_cols(gate_grad, w_gate) + contract_cols(up_grad, w_up)).astype(jnp.bfloat16),
        "fsdp",
        scatter_dimension=0,
        tiled=True,
    )
    grad_tokens = summed[None]
    return (grad_tokens, grad_gate, grad_up, grad_down)


def solution(mesh):
    return jax.shard_map(
        body,
        mesh=mesh,
        in_specs=(
            P("lang", "fsdp", None),
            P("lang", "fsdp", None),
            P("lang", None),
            P(None, "fsdp"),
            P(None, "fsdp"),
            P("fsdp", None),
        ),
        out_specs=(
            P("lang", "fsdp", None),
            P("lang", "fsdp"),
            P("lang", "fsdp"),
            P("fsdp", "lang"),
        ),
        check_vma=False,
    )
```

profile of v0, /device:TPU:0, one launch (start us, length us, event | category | flops | bytes accessed | tf_op | source)
XLA Modules:
  0.0 516.3 jit_solution(6174130623956002040)
XLA Ops:
  7.2 0.0 all-gather.2.cloned.1.call-start
  7.2 2.7 pad_maximum_fusion
  10.0 0.0 all-gather.2.cloned.1.call-update
  10.0 0.0 reduce-scatter.2.cloned.1.call-start
  10.0 0.7 reduce.5
  10.7 0.4 convert_reduce_fusion
  11.1 150.3 %all-gather.2.cloned.1.call-done = bf16[2,768,8192]{2,1,0:T(8,128)(2,1)} async-done(((bf16[2,48,8192]{2,1,0:T(8,128)(2,1)}), bf16[2,768,8192]{2,1,0:T(8,128)(2,1)}) %all-gather.2.cloned.1.call-update) | async-done | bytes 25165840 | tf_op jit(solution)/shard_map/all_gather | solution.py:11
  161.4 7.8 %fusion.6 = f32[768,256]{1,0:T(8,128)S(1)} fusion(bf16[8192,256]{1,0:T(8,128)(2,1)} %param.9, bf16[2,768,8192]{2,1,0:T(8,128)(2,1)} %all-gather.2.cloned.1.call-done), kind=kOutput, calls=%fused_computation.11 | convolution fusion | flops 3221225472 | bytes 17563648 | tf_op jit(solution)/shard_map/dot_general | solution.py:49
  169.2 0.0 copy-done.3
  169.2 0.0 copy-start.4
  169.2 6.6 %fusion.7 = f32[768,256]{1,0:T(8,128)S(1)} fusion(bf16[8192,256]{1,0:T(8,128)(2,1)S(1)} %copy-done.3, bf16[2,768,8192]{2,1,0:T(8,128)(2,1)} %all-gather.2.cloned.1.call-done), kind=kOutput, calls=%fused_computation.12 | convolution fusion | flops 3221225472 | bytes 17563648 | tf_op jit(solution)/shard_map/dot_general | solution.py:50
  175.7 0.0 copy-done.4
  175.8 0.0 copy-start.2
  175.8 8.4 %multiply_convert_fusion.1 = (bf16[768,256]{1,0:T(8,128)(2,1)S(1)}, bf16[768,256]{1,0:T(8,128)(2,1)S(1)}) fusion(f32[768,256]{1,0:T(8,128)S(1)} %fusion.6, f32[768,256]{1,0:T(8,128)S(1)} %fusion.7, f32[768]{0:T(1024)S(1)} %broadcast_divide_fusion, bf16[256,8192]{1,0:T(8,128)(2,1)S(1)} %copy-done.4, bf16[2,768,8192]{2,1,0:T(8,128)(2,1)} %all-gather.2.cloned.1.call-done), kind=kOutput, calls=%fused_computation.17 | convolution fusion | flops 3223977984 | bytes 19139584 | tf_op jit(solution)/shard_map/dot_general | solution.py:36
  184.2 0.0 copy-done.2
  184.2 10.0 %fusion.15 = f32[768,8192]{1,0:T(8,128)} fusion(bf16[768,256]{1,0:T(8,128)(2,1)S(1)} %get-tuple-element.32, bf16[8192,256]{1,0:T(8,128)(2,1)S(1)} %copy-done.2), kind=kOutput, calls=%fused_computation.30 | convolution fusion | flops 3221225472 | bytes 29753344 | tf_op jit(solution)/shard_map/dot_general | solution.py:36
  194.2 15.6 %add_convert_fusion = bf16[768,8192]{1,0:T(8,128)(2,1)} fusion(f32[768,8192]{1,0:T(8,128)} %fusion.15, bf16[768,256]{1,0:T(8,128)(2,1)S(1)} %get-tuple-element.31, bf16[8192,256]{1,0:T(8,128)(2,1)} %param.10), kind=kOutput, calls=%fused_computation.4 | convolution fusion | flops 3233808384 | bytes 42336256 | tf_op jit(solution)/shard_map/dot_general | solution.py:36
  209.8 0.0 reduce-scatter.2.cloned.1.call-update
  209.8 6.7 %fusion.4 = f32[8192,256]{1,0:T(8,128)S(1)} fusion(bf16[768,256]{1,0:T(8,128)(2,1)S(1)} %get-tuple-element.31, bf16[2,768,8192]{2,1,0:T(8,128)(2,1)} %all-gather.2.cloned.1.call-done), kind=kOutput, calls=%fused_computation.9 | convolution fusion | flops 3221225472 | bytes 21364736 | tf_op jit(solution)/shard_map/dot_general | solution.py:30
  216.5 0.0 copy-start
  216.5 11.2 %fusion.5 = f32[8192,256]{1,0:T(8,128)S(1)} fusion(bf16[768,256]{1,0:T(8,128)(2,1)S(1)} %get-tuple-element.32, bf16[2,768,8192]{2,1,0:T(8,128)(2,1)} %all-gather.2.cloned.1.call-done), kind=kOutput, calls=%fused_computation.10 | convolution fusion | flops 3221225472 | bytes 21364736 | tf_op jit(solution)/shard_map/dot_general | solution.py:30
  227.7 15.7 %fusion.2 = f32[8192,256]{1,0:T(8,128)} fusion(bf16[2,768,8192]{2,1,0:T(8,128)(2,1)} %all-gather.2.cloned.1.call-done, f32[768,256]{1,0:T(8,128)S(1)} %fusion.7, f32[768]{0:T(1024)S(1)} %broadcast_divide_fusion, f32[768,256]{1,0:T(8,128)S(1)} %fusion.6), kind=kOutput, calls=%fused_computation.7 | convolution fusion | flops 3222601728 | bytes 22547456 | tf_op jit(solution)/shard_map/dot_general | solution.py:30
  243.4 0.0 copy-done
  243.4 8.9 %fusion.1 = f32[256]{0:T(256)S(1)} fusion(f32[1,8192,256]{2,1,0:T(8,128)} %bitcast.44, f32[1,8192,256]{2,1,0:T(8,128)S(1)} %bitcast.40, f32[1,8192,256]{2,1,0:T(8,128)S(1)} %bitcast.42), kind=kLoop, calls=%fused_computation.3 | loop fusion | flops 25165568 | bytes 25166848 | tf_op jit(solution)/shard_map/reduce_sum | solution.py:66
  252.4 10.7 %all_to_all.15 = f32[8,1,256]{2,1,0:T(1,128)S(1)} all-to-all(f32[8,1,256]{2,1,0:T(1,128)S(1)} %broadcast_in_dim.5), channel_id=1, replica_groups=mesh['lang'=8,'fsdp'=16] {'lang'}, dimensions={0} | all-to-all | bytes 16384 | tf_op jit(solution)/shard_map/all_to_all | solution.py:20
  263.1 13.7 %fusion = bf16[1,3,8192,256]{3,2,1,0:T(8,128)(2,1)} fusion(f32[1,1,8192,256]{3,2,1,0:T(8,128)} %bitcast.45, f32[1,1,8192,256]{3,2,1,0:T(8,128)} %bitcast.41, f32[1,1,8192,256]{3,2,1,0:T(8,128)} %bitcast.43, f32[256]{0:T(256)S(1)} %multiply_divide_fusion), kind=kLoop, calls=%fused_computation.1 | loop fusion | flops 25165824 | bytes 37749760 | tf_op jit(solution)/shard_map/convert_element_type | solution.py:71
  276.7 17.9 %copy.20 = bf16[1,3,8192,256]{3,1,0,2:T(4,128)(2,1)S(1)} copy(bf16[1,3,8192,256]{3,2,1,0:T(8,128)(2,1)} %fusion) | data formatting | bytes 25165824 | tf_op jit(solution)/shard_map/convert_element_type | solution.py:71
  294.6 196.0 %all_to_all.16 = bf16[1,3,8192,256]{3,1,0,2:T(4,128)(2,1)} all-to-all(bf16[1,3,8192,256]{3,1,0,2:T(4,128)(2,1)S(1)} %copy.20), channel_id=1, replica_groups=mesh['lang'=8,'fsdp'=16] {'lang'}, dimensions={2} | all-to-all | bytes 25165824 | tf_op jit(solution)/shard_map/all_to_all | solution.py:70
  490.6 9.7 %reduce.4 = bf16[3,1024,256]{2,0,1:T(4,128)(2,1)S(1)} reduce(bf16[3,8,1024,256]{3,0,2,1:T(4,128)(2,1)} %bitcast.39, bf16[]{:T(256)} %constant.14), dimensions={1}, to_apply=%region_4.0.clone | reduce | flops 5505024 | bytes 14155778 | tf_op jit(solution)/shard_map/reduce_sum | solution.py:73
  500.3 3.3 fusion.14
  503.6 3.5 copy.26
  507.1 2.4 copy_bitcast_fusion
  (9 shorter events, 0.1 us)
Async XLA Ops:
  7.2 154.2 %all-gather.2.cloned.1.call-start = ((), (), s32[]{:S(2)}) async-start(), calls=%async_computation.3 | async-start | bytes 26738688 | tf_op jit(solution)/shard_map/all_gather | solution.py:11
  10.0 499.5 %reduce-scatter.2.cloned.1.call-start = ((), (), s32[]{:S(2)}) async-start(), calls=%async_computation.4 | async-start | bytes 13369344 | tf_op jit(solution)/shard_map/reduce_scatter | solution.py:77
  161.4 7.8 %copy-start.3 = (bf16[8192,256]{1,0:T(8,128)(2,1)S(1)}, bf16[8192,256]{1,0:T(8,128)(2,1)}, u32[]{:S(2)}) copy-start(bf16[8192,256]{1,0:T(8,128)(2,1)} %param.10) | copy-start | bytes 12582916
  169.2 6.6 %copy-start.4 = (bf16[256,8192]{1,0:T(8,128)(2,1)S(1)}, bf16[256,8192]{1,0:T(8,128)(2,1)}, u32[]{:S(2)}) copy-start(bf16[256,8192]{1,0:T(8,128)(2,1)} %param.11) | copy-start | bytes 12582916
  175.8 8.4 %copy-start.2 = (bf16[8192,256]{1,0:T(8,128)(2,1)S(1)}, bf16[8192,256]{1,0:T(8,128)(2,1)}, u32[]{:S(2)}) copy-start(bf16[8192,256]{1,0:T(8,128)(2,1)} %param.9) | copy-start | bytes 12582916
  216.5 26.9 %copy-start = (f32[8192,256]{1,0:T(8,128)}, f32[8192,256]{1,0:T(8,128)S(1)}, u32[]{:S(2)}) copy-start(f32[8192,256]{1,0:T(8,128)S(1)} %fusion.4) | copy-start | bytes 25165828
  227.7 15.7 %copy-start.1 = (f32[8192,256]{1,0:T(8,128)}, f32[8192,256]{1,0:T(8,128)S(1)}, u32[]{:S(2)}) copy-start(f32[8192,256]{1,0:T(8,128)S(1)} %fusion.5) | copy-start | bytes 25165828
Sparse Core Ops, SparseCore 0:
  10.4 150.9 all-gather.1
  210.0 128.4 reduce-scatter.1
where the time goes:
time: 517 us; the launch traced here: 516 us
  blocking collectives  207 us (40%)
  waiting for transfers between devices  150 us (29%)
  matrix products  81.9 us (16%)
  other arithmetic  36.2 us (7%)
  local copies, waits for them, and re-layouts  27 us (5%)
  between operations  14.2 us (3%)
    all_to_all x1, blocking collectives, body(): lax.all_to_all(weighted.astype(jnp.bfloat16)[None], 'lang', split_axis=2,...  196 us
    all_gather x1, waiting for transfers between devices, sent_together(): lax.all_gather(both, axis, axis=dim, tiled=True)  150 us
    dot_general x3, matrix products, contract_cols(): lax.dot_general(left, right, (((1,), (1,)), ((), ())), preferred_element_...  34 us
    dot_general x3, matrix products, contract_rows(): lax.dot_general(left, right, (((0,), (0,)), ((), ())), preferred_element_...  33.5 us
    convert_element_type x1, local copies, waits for them, and re-layouts, body(): weighted.astype(jnp.bfloat16)[None]  17.9 us
    convert_element_type x1, other arithmetic, body(): weighted.astype(jnp.bfloat16)[None]  13.7 us
    all_to_all x1, blocking collectives, copy_for_each(): lax.all_to_all(jnp.broadcast_to(value[None], (length, *value.shape)), axi...  10.7 us
  transfers between devices with their start and end apart: 2, of which 1 were waited for; matrix products, arithmetic and copies ran while one was open for 18% of the time, Pallas kernels for 0%

commit v1 on v0

--- a/solution.py
+++ b/solution.py
@@ -67,8 +67,16 @@
     ratios = 1.0 / moment
     summed_ratio = taken_together(ratios, "lang")
     weighted = stacked * (ratios / summed_ratio)[None, None, :]
-    pieces = lax.all_to_all(
-        weighted.astype(jnp.bfloat16)[None], "lang", split_axis=2, concat_axis=0, tiled=True
+    pieces = jnp.concatenate(
+        lax.all_to_all(
+            jnp.stack(
+                jnp.split(weighted.astype(jnp.bfloat16)[None], lax.axis_size("lang"), axis=2)
+            ),
+            "lang",
+            0,
+            0,
+        ),
+        axis=0,
     )
     shares = jnp.sum(pieces, axis=0, dtype=jnp.float32)
     grad_gate = shares[0].astype(jnp.bfloat16)

time: 517 us -> 456 us (0.88)
  blocking collectives: 207 us -> 177 us
  local copies, waits for them, and re-layouts: 27 us -> 2.93 us
  other arithmetic: 36.2 us -> 29 us
    all_to_all x1, blocking collectives: 196 us -> 166 us  [body(): lax.all_to_all(jnp.stack(jnp.split(weighted.astype(jnp.bfloat16)[None], l...]
    convert_element_type x1 -> x0, local copies, waits for them, and re-layouts: 17.9 us -> none  [body(): weighted.astype(jnp.bfloat16)[None]]
  transfers between devices with their start and end apart: 2 -> 2, of which waited for: 1 -> 1; matrix products, arithmetic and copies ran while one was open for 18% -> 14% of each run, Pallas kernels for 0% -> 0%
where the time goes in v1:
time: 456 us; the launch traced here: 455 us
  blocking collectives  177 us (39%)
  waiting for transfers between devices  150 us (33%)
  matrix products  82.2 us (18%)
  other arithmetic  29 us (6%)
  between operations  14.2 us (3%)
    all_to_all x1, blocking collectives, body(): lax.all_to_all(jnp.stack(jnp.split(weighted.astype(jnp.bfloat16)[None], l...  166 us
    all_gather x1, waiting for transfers between devices, sent_together(): lax.all_gather(both, axis, axis=dim, tiled=True)  150 us
    dot_general x3, matrix products, contract_cols(): lax.dot_general(left, right, (((1,), (1,)), ((), ())), preferred_element_...  34 us
    dot_general x3, matrix products, contract_rows(): lax.dot_general(left, right, (((0,), (0,)), ((), ())), preferred_element_...  33.8 us
    all_to_all x1, blocking collectives, copy_for_each(): lax.all_to_all(jnp.broadcast_to(value[None], (length, *value.shape)), axi...  10.7 us
    convert_element_type x1, other arithmetic, body(): weighted.astype(jnp.bfloat16)[None]  9.59 us
  transfers between devices with their start and end apart: 2, of which 1 were waited for; matrix products, arithmetic and copies ran while one was open for 14% of the time, Pallas kernels for 0%

profile of v1, /device:TPU:0, one launch (start us, length us, event | category | flops | bytes accessed | tf_op | source)
XLA Modules:
  0.0 455.4 jit_solution(43791852890391510)
XLA Ops:
  7.2 0.0 all-gather.2.cloned.1.call-start
  7.2 2.7 pad_maximum_fusion
  10.0 0.0 all-gather.2.cloned.1.call-update
  10.0 0.0 reduce-scatter.2.cloned.1.call-start
  10.0 0.7 reduce.3
  10.7 0.4 convert_reduce_fusion
  11.1 150.3 %all-gather.2.cloned.1.call-done = bf16[2,768,8192]{2,1,0:T(8,128)(2,1)} async-done(((bf16[2,48,8192]{2,1,0:T(8,128)(2,1)}), bf16[2,768,8192]{2,1,0:T(8,128)(2,1)}) %all-gather.2.cloned.1.call-update) | async-done | bytes 25165840 | tf_op jit(solution)/shard_map/all_gather | solution.py:11
  161.4 7.8 %fusion.6 = f32[768,256]{1,0:T(8,128)S(1)} fusion(bf16[8192,256]{1,0:T(8,128)(2,1)} %param.9, bf16[2,768,8192]{2,1,0:T(8,128)(2,1)} %all-gather.2.cloned.1.call-done), kind=kOutput, calls=%fused_computation.11 | convolution fusion | flops 3221225472 | bytes 17563648 | tf_op jit(solution)/shard_map/dot_general | solution.py:49
  169.2 0.0 copy-start.4
  169.2 6.6 %fusion.7 = f32[768,256]{1,0:T(8,128)S(1)} fusion(bf16[8192,256]{1,0:T(8,128)(2,1)S(1)} %copy-done.3, bf16[2,768,8192]{2,1,0:T(8,128)(2,1)} %all-gather.2.cloned.1.call-done), kind=kOutput, calls=%fused_computation.12 | convolution fusion | flops 3221225472 | bytes 17563648 | tf_op jit(solution)/shard_map/dot_general | solution.py:50
  175.8 8.4 %multiply_convert_fusion.1 = (bf16[768,256]{1,0:T(8,128)(2,1)S(1)}, bf16[768,256]{1,0:T(8,128)(2,1)S(1)}) fusion(f32[768,256]{1,0:T(8,128)S(1)} %fusion.6, f32[768,256]{1,0:T(8,128)S(1)} %fusion.7, f32[768]{0:T(1024)S(1)} %broadcast_divide_fusion, bf16[256,8192]{1,0:T(8,128)(2,1)S(1)} %copy-done.4, bf16[2,768,8192]{2,1,0:T(8,128)(2,1)} %all-gather.2.cloned.1.call-done), kind=kOutput, calls=%fused_computation.33 | convolution fusion | flops 3223977984 | bytes 19139584 | tf_op jit(solution)/shard_map/dot_general | solution.py:36
  184.2 10.0 %fusion.22 = f32[768,8192]{1,0:T(8,128)} fusion(bf16[768,256]{1,0:T(8,128)(2,1)S(1)} %get-tuple-element.20, bf16[8192,256]{1,0:T(8,128)(2,1)S(1)} %copy-done.2), kind=kOutput, calls=%fused_computation.46 | convolution fusion | flops 3221225472 | bytes 29753344 | tf_op jit(solution)/shard_map/dot_general | solution.py:36
  194.2 15.6 %add_convert_fusion = bf16[768,8192]{1,0:T(8,128)(2,1)} fusion(f32[768,8192]{1,0:T(8,128)} %fusion.22, bf16[768,256]{1,0:T(8,128)(2,1)S(1)} %get-tuple-element.19, bf16[8192,256]{1,0:T(8,128)(2,1)} %param.10), kind=kOutput, calls=%fused_computation.4 | convolution fusion | flops 3233808384 | bytes 42336256 | tf_op jit(solution)/shard_map/dot_general | solution.py:36
  209.8 0.0 reduce-scatter.2.cloned.1.call-update
  209.8 7.3 %fusion.2 = f32[8192,256]{1,0:T(8,128)S(1)} fusion(bf16[2,768,8192]{2,1,0:T(8,128)(2,1)} %all-gather.2.cloned.1.call-done, f32[768,256]{1,0:T(8,128)S(1)} %fusion.7, f32[768]{0:T(1024)S(1)} %broadcast_divide_fusion, f32[768,256]{1,0:T(8,128)S(1)} %fusion.6), kind=kOutput, calls=%fused_computation.7 | convolution fusion | flops 3222601728 | bytes 22547456 | tf_op jit(solution)/shard_map/dot_general | solution.py:30
  217.1 11.2 %fusion.4 = f32[8192,256]{1,0:T(8,128)S(1)} fusion(bf16[768,256]{1,0:T(8,128)(2,1)S(1)} %get-tuple-element.19, bf16[2,768,8192]{2,1,0:T(8,128)(2,1)} %all-gather.2.cloned.1.call-done), kind=kOutput, calls=%fused_computation.9 | convolution fusion | flops 3221225472 | bytes 21364736 | tf_op jit(solution)/shard_map/dot_general | solution.py:30
  228.3 15.3 %fusion.5 = f32[8192,256]{1,0:T(8,128)} fusion(bf16[768,256]{1,0:T(8,128)(2,1)S(1)} %get-tuple-element.20, bf16[2,768,8192]{2,1,0:T(8,128)(2,1)} %all-gather.2.cloned.1.call-done), kind=kOutput, calls=%fused_computation.10 | convolution fusion | flops 3221225472 | bytes 21364736 | tf_op jit(solution)/shard_map/dot_general | solution.py:30
  243.7 8.9 %fusion.1 = f32[256]{0:T(256)S(1)} fusion(f32[1,8192,256]{2,1,0:T(8,128)S(1)} %bitcast.70, f32[1,8192,256]{2,1,0:T(8,128)S(1)} %bitcast.72, f32[1,8192,256]{2,1,0:T(8,128)} %bitcast.74), kind=kLoop, calls=%fused_computation.3 | loop fusion | flops 25165568 | bytes 25166848 | tf_op jit(solution)/shard_map/reduce_sum | solution.py:66
  252.6 10.7 %all_to_all.11 = f32[8,1,256]{2,1,0:T(1,128)S(1)} all-to-all(f32[8,1,256]{2,1,0:T(1,128)S(1)} %broadcast_in_dim.5), channel_id=1, replica_groups=mesh['lang'=8,'fsdp'=16] {'lang'}, dimensions={0} | all-to-all | bytes 16384 | tf_op jit(solution)/shard_map/all_to_all | solution.py:20
  263.4 9.6 %fusion = bf16[1,3,8192,256]{3,2,1,0:T(8,128)(2,1)S(1)} fusion(f32[1,1,8192,256]{3,2,1,0:T(8,128)} %bitcast.71, f32[1,1,8192,256]{3,2,1,0:T(8,128)} %bitcast.73, f32[1,1,8192,256]{3,2,1,0:T(8,128)} %bitcast.75, f32[256]{0:T(256)S(1)} %multiply_divide_fusion), kind=kLoop, calls=%fused_computation.1 | loop fusion | flops 25165824 | bytes 37749760 | tf_op jit(solution)/shard_map/convert_element_type | solution.py:73
  273.0 0.1 fusion.15
  273.1 0.1 fusion.14
  273.2 0.1 fusion.13
  273.3 0.1 fusion.12
  273.4 0.1 fusion.11
  273.5 0.1 fusion.10
  273.6 0.1 fusion.9
  273.8 0.1 fusion.8
  273.9 166.0 %all_to_all.12 = bf16[8,1,3,1024,256]{4,3,2,1,0:T(8,128)(2,1)} all-to-all(bf16[8,1,3,1024,256]{4,3,2,1,0:T(8,128)(2,1)S(1)} %fusion.8), channel_id=1, replica_groups=mesh['lang'=8,'fsdp'=16] {'lang'}, dimensions={0} | all-to-all | bytes 25165824 | tf_op jit(solution)/shard_map/all_to_all | solution.py:71
  439.9 6.6 %reduce.2 = bf16[3,1024,256]{2,1,0:T(8,128)(2,1)S(1)} reduce(bf16[8,1,3,1024,256]{4,3,2,1,0:T(8,128)(2,1)} %all_to_all.12, bf16[]{:T(256)} %constant.14), dimensions={0,1}, to_apply=%region_4.0.clone | reduce | flops 5505024 | bytes 14155778 | tf_op jit(solution)/shard_map/reduce_sum | solution.py:81
  446.5 1.1 slice_bitcast_fusion.18
  447.6 1.0 copy.13
  (15 shorter events, 0.1 us)
Async XLA Ops:
  7.2 154.2 %all-gather.2.cloned.1.call-start = ((), (), s32[]{:S(2)}) async-start(), calls=%async_computation.3 | async-start | bytes 26738688 | tf_op jit(solution)/shard_map/all_gather | solution.py:11
  10.0 438.6 %reduce-scatter.2.cloned.1.call-start = ((), (), s32[]{:S(2)}) async-start(), calls=%async_computation.4 | async-start | bytes 13369344 | tf_op jit(solution)/shard_map/reduce_scatter | solution.py:85
  161.4 7.8 %copy-start.3 = (bf16[8192,256]{1,0:T(8,128)(2,1)S(1)}, bf16[8192,256]{1,0:T(8,128)(2,1)}, u32[]{:S(2)}) copy-start(bf16[8192,256]{1,0:T(8,128)(2,1)} %param.10) | copy-start | bytes 12582916
  169.2 6.6 %copy-start.4 = (bf16[256,8192]{1,0:T(8,128)(2,1)S(1)}, bf16[256,8192]{1,0:T(8,128)(2,1)}, u32[]{:S(2)}) copy-start(bf16[256,8192]{1,0:T(8,128)(2,1)} %param.11) | copy-start | bytes 12582916
  175.8 8.4 %copy-start.2 = (bf16[8192,256]{1,0:T(8,128)(2,1)S(1)}, bf16[8192,256]{1,0:T(8,128)(2,1)}, u32[]{:S(2)}) copy-start(bf16[8192,256]{1,0:T(8,128)(2,1)} %param.9) | copy-start | bytes 12582916
  217.1 26.6 %copy-start = (f32[8192,256]{1,0:T(8,128)}, f32[8192,256]{1,0:T(8,128)S(1)}, u32[]{:S(2)}) copy-start(f32[8192,256]{1,0:T(8,128)S(1)} %fusion.2) | copy-start | bytes 25165828
  228.3 15.3 %copy-start.1 = (f32[8192,256]{1,0:T(8,128)}, f32[8192,256]{1,0:T(8,128)S(1)}, u32[]{:S(2)}) copy-start(f32[8192,256]{1,0:T(8,128)S(1)} %fusion.4) | copy-start | bytes 25165828
Sparse Core Ops, SparseCore 0:
  10.4 150.9 all-gather.1
  210.0 146.3 reduce-scatter.1
